TPU v7x, 512 devices: a whole 4x4x16 slice. The times are simulated.
512 devices in a mesh: dp: 4 (over z_lo), row: 8 (over y, core), col: 16 (over z_hi, x).
Axes of the slice: x: 4, y: 4, z: 16 (z_hi: 4, z_lo: 4; z = z_hi * 4 + z_lo), core: 2. Of those that a mesh axis runs over, the one named last changes fastest.
Arguments:
- queries: bfloat16 [4, 64, 256, 768], P('dp', 'row', 'col'), may hold values from -5.5 to 5.5
- keys: bfloat16 [4, 64, 256, 768], P('dp', 'row', 'col'), may hold values from -5.5 to 5.5
- values: bfloat16 [4, 64, 256, 768], P('dp', 'row', 'col'), may hold values from -6 to 6
- occupancy: int32 [4, 8, 32], P('dp', 'row', 'col'), may hold values from 0 to 64, as said below
- out_weight: bfloat16 [768, 768], P('dp'), may hold values from -0.21875 to 0.21875
- grad_out: bfloat16 [4, 64, 256, 768], P('dp', 'row', 'col'), may hold values from -6 to 6
Outputs:
- grad_queries: bfloat16 [4, 64, 256, 768], P('dp', 'row', 'col')
- grad_keys: bfloat16 [4, 64, 256, 768], P('dp', 'row', 'col')
- grad_values: bfloat16 [4, 64, 256, 768], P('dp', 'row', 'col')
- grad_weight: float32 [768, 768], P('dp')
Inputs may be any that keep to these rules, and one draw needn't show every extreme that they name: `occupancy`: the occupied tiles of a block are its first that many tiles, row by row over its 8 x 8 tiles. Every slide has a block holding 8 * 8 and a block holding 0.
All inputs are finite; a program needn't handle non-finite values.
Results may differ from a plain program's by a relative error of at most 0.02.
Values may be sent and summed in bfloat16 or wider, within the bound.
A program may use at most 64 MiB of HBM per device.

v0:
```python
import jax
import jax.numpy as jnp
from jax import lax
from jax.sharding import PartitionSpec as P

HEAD_DIM = 64
SIDE = 8
REACH = 3
NEG = -1e30


def passed_along(value, axis, steps):
    count = lax.axis_size(axis)
    leading, last = (max(0, -steps), min(count, count - steps))
    return lax.ppermute(value, axis, [(source, source + steps) for source in range(leading, last)])


def for_sending(value):
    return jax.tree.map(lambda a: a.astype(jnp.bfloat16) if a.dtype == jnp.float32 else a, value)


def extended(cells, sides, width):
    for axis, dim in sides:
        count = lax.axis_size(axis)
        ends = count - 1
        head = lax.slice_in_dim(cells, 0, width, axis=dim)
        tail = lax.slice_in_dim(cells, cells.shape[dim] - width, cells.shape[dim], axis=dim)
        cells = jnp.concatenate(
            [
                lax.ppermute(tail, axis, [(i, (i + 1) % count) for i in range(ends)]),
                cells,
                lax.ppermute(head, axis, [((i + 1) % count, i) for i in range(ends)]),
            ],
            axis=dim,
        )
    return cells


def product(form, left, right):
    return jnp.einsum(form, left, right, preferred_element_type=jnp.float32)


def near_table(block_side, radius):
    window = block_side + 2 * radius
    queries_at = jnp.arange(block_side * block_side)
    keys_at = jnp.arange(window * window)
    row_gap = keys_at[None, :] // window - queries_at[:, None] // block_side - radius
    col_gap = keys_at[None, :] % window - queries_at[:, None] % block_side - radius
    return (jnp.abs(row_gap) <= radius) & (jnp.abs(col_gap) <= radius)


def tile_valid(counts, block_side):
    inside = jnp.arange(block_side * block_side, dtype=jnp.int32).reshape(block_side, block_side)
    flags = inside[None, :, None, :] < counts[:, None, :, None]
    return flags.reshape(counts.shape[0] * block_side, counts.shape[1] * block_side).astype(
        jnp.float32
    )


def blockify(source, block_side):
    height, breadth = (source.shape[0], source.shape[1])
    others = source.shape[2:]
    shaped = source.reshape(
        (height // block_side, block_side, breadth // block_side, block_side) + others
    )
    shaped = jnp.swapaxes(shaped, 1, 2)
    return shaped.reshape(
        (height // block_side, breadth // block_side, block_side * block_side) + others
    )


def unblock(source, block_side):
    block_rows, block_cols = (source.shape[0], source.shape[1])
    others = source.shape[3:]
    shaped = source.reshape((block_rows, block_cols, block_side, block_side) + others)
    shaped = jnp.swapaxes(shaped, 1, 2)
    return shaped.reshape((block_rows * block_side, block_cols * block_side) + others)


def cut_axis(source, dimension, block_side, radius, number):
    padding = [(0, 0)] * source.ndim
    padding[dimension] = (0, block_side - 2 * radius)
    shaped = jnp.pad(source, padding)
    shaped = shaped.reshape(
        source.shape[:dimension] + (number + 1, block_side) + source.shape[dimension + 1 :]
    )
    leading = lax.slice_in_dim(shaped, 0, number, axis=dimension)
    trailing = lax.slice_in_dim(
        lax.slice_in_dim(shaped, 1, number + 1, axis=dimension), 0, 2 * radius, axis=dimension + 1
    )
    return jnp.concatenate([leading, trailing], axis=dimension + 1)


def windows(source, block_side, radius, block_rows, block_cols):
    window = block_side + 2 * radius
    shaped = cut_axis(source, 0, block_side, radius, block_rows)
    shaped = cut_axis(shaped, 2, block_side, radius, block_cols)
    shaped = jnp.swapaxes(shaped, 1, 2)
    return shaped.reshape((block_rows * block_cols, window * window) + source.shape[2:])


def merge_axis(source, dimension, block_side, radius, number):
    leading = lax.slice_in_dim(source, 0, block_side, axis=dimension + 1)
    trailing = lax.slice_in_dim(source, block_side, block_side + 2 * radius, axis=dimension + 1)
    lead_pad = [(0, 0)] * source.ndim
    lead_pad[dimension] = (0, 1)
    trail_pad = [(0, 0)] * source.ndim
    trail_pad[dimension] = (1, 0)
    trail_pad[dimension + 1] = (0, block_side - 2 * radius)
    summed = jnp.pad(leading, lead_pad) + jnp.pad(trailing, trail_pad)
    summed = summed.reshape(
        source.shape[:dimension] + ((number + 1) * block_side,) + source.shape[dimension + 2 :]
    )
    return lax.slice_in_dim(summed, 0, number * block_side + 2 * radius, axis=dimension)


def fold_back(source, block_side, radius, block_rows, block_cols):
    window = block_side + 2 * radius
    shaped = source.reshape((block_rows, block_cols, window, window) + source.shape[2:])
    shaped = jnp.swapaxes(shaped, 1, 2)
    shaped = merge_axis(shaped, 2, block_side, radius, block_cols)
    return merge_axis(shaped, 0, block_side, radius, block_rows)


def attend(query_blocks, key_win, value_win, key_flag, query_flag, nearby, scaling):
    scores = product("nqhd,nkhd->nhqk", query_blocks, key_win) * scaling
    allowed = nearby[None, None] & (key_flag[:, None, None, :] > 0)
    masked = jnp.where(allowed, scores, NEG)
    highest = jnp.max(masked, axis=-1, keepdims=True)
    raised = jnp.exp(masked - highest)
    inverse = 1.0 / jnp.sum(raised, axis=-1, keepdims=True)
    weights = raised * inverse
    rounded = weights.astype(jnp.bfloat16)
    mixed = product("nhqk,nkhd->nqhd", rounded, value_win)
    attended = (mixed * query_flag[:, :, None, None]).astype(jnp.bfloat16)
    return (attended, weights, rounded, highest, inverse)


def query_side(weights, grad_blocks, key_win, value_win, scaling):
    prob_grad = product("nqhd,nkhd->nhqk", grad_blocks, value_win)
    correction = jnp.sum(weights * prob_grad, axis=-1, keepdims=True)
    score_grad = (weights * (prob_grad - correction) * scaling).astype(jnp.bfloat16)
    query_grad = product("nhqk,nkhd->nqhd", score_grad, key_win)
    return (query_grad, score_grad, correction)


def return_rims(key_full, value_full):
    middle = (key_full[REACH:-REACH], value_full[REACH:-REACH])
    for offset in (1, -1):
        if offset == 1:
            border = (key_full[-REACH:], value_full[-REACH:])
        else:
            border = (key_full[:REACH], value_full[:REACH])
        arrived = (
            passed_along(border[0].astype(jnp.bfloat16), "row", offset).astype(jnp.float32),
            passed_along(border[1].astype(jnp.bfloat16), "row", offset).astype(jnp.float32),
        )
        if offset == 1:
            middle = tuple(
                (portion.at[:REACH].add(incoming) for portion, incoming in zip(middle, arrived))
            )
        else:
            middle = tuple(
                (portion.at[-REACH:].add(incoming) for portion, incoming in zip(middle, arrived))
            )
    centre = tuple((portion[:, REACH:-REACH] for portion in middle))
    for offset in (1, -1):
        if offset == 1:
            border = tuple((portion[:, -REACH:] for portion in middle))
        else:
            border = tuple((portion[:, :REACH] for portion in middle))
        arrived = jax.tree.map(
            lambda part, own: part.astype(own.dtype),
            passed_along(for_sending(border), "col", offset),
            border,
        )
        if offset == 1:
            centre = tuple(
                (portion.at[:, :REACH].add(incoming) for portion, incoming in zip(centre, arrived))
            )
        else:
            centre = tuple(
                (portion.at[:, -REACH:].add(incoming) for portion, incoming in zip(centre, arrived))
            )
    return centre


def on_device(queries, keys, values, occupancy, out_weight, grad_out):
    query_tiles = queries[0]
    key_tiles = keys[0]
    value_tiles = values[0]
    grad_tiles = grad_out[0]
    counts = occupancy[0]
    height, breadth, channels = query_tiles.shape
    out_width = grad_tiles.shape[2]
    head_count = channels // HEAD_DIM
    block_rows = height // SIDE
    block_cols = breadth // SIDE
    block_count = block_rows * block_cols
    block_area = SIDE * SIDE
    window = SIDE + 2 * REACH
    window_area = window * window
    tile_count = height * breadth
    nearby = near_table(SIDE, REACH)
    scaling = HEAD_DIM ** (-0.5)
    occupied = tile_valid(counts, SIDE)
    key_ext, value_ext, flag_ext = (
        extended(key_tiles, (("row", 0), ("col", 1)), REACH),
        extended(value_tiles, (("row", 0), ("col", 1)), REACH),
        extended(occupied.astype(jnp.bfloat16), (("row", 0), ("col", 1)), REACH),
    )
    key_win = windows(key_ext, SIDE, REACH, block_rows, block_cols).reshape(
        block_count, window_area, head_count, HEAD_DIM
    )
    value_win = windows(value_ext, SIDE, REACH, block_rows, block_cols).reshape(
        block_count, window_area, head_count, HEAD_DIM
    )
    flag_win = windows(flag_ext, SIDE, REACH, block_rows, block_cols)
    query_blocks = blockify(query_tiles, SIDE).reshape(
        block_count, block_area, head_count, HEAD_DIM
    )
    query_flag = blockify(occupied, SIDE).reshape(block_count, block_area)
    attended, weights, rounded, highest, inverse = attend(
        query_blocks, key_win, value_win, flag_win, query_flag, nearby, scaling
    )
    flat_grads = grad_tiles.reshape(tile_count, out_width)
    out_back = lax.dot_general(
        flat_grads,
        lax.all_gather(out_weight, "dp", axis=0, tiled=True),
        (((1,), (1,)), ((), ())),
        preferred_element_type=jnp.float32,
    )
    gated_grad = out_back.astype(jnp.bfloat16).reshape(height, breadth, channels) * occupied[
        :, :, None
    ].astype(jnp.bfloat16)
    grad_blocks = blockify(gated_grad, SIDE).reshape(block_count, block_area, head_count, HEAD_DIM)
    out_blocks = blockify(grad_tiles, SIDE).reshape(tile_count, out_width)
    weight_term = lax.dot_general(
        attended.reshape(tile_count, channels),
        out_blocks,
        (((0,), (0,)), ((), ())),
        preferred_element_type=jnp.float32,
    )
    summed = lax.psum(weight_term, ("row", "col"))
    slide_part = lax.psum_scatter(
        summed.astype(jnp.bfloat16), "dp", scatter_dimension=0, tiled=True
    ).astype(jnp.float32)
    all_tiles = tile_count * lax.axis_size("dp") * lax.axis_size("row") * lax.axis_size("col")
    grad_weight = slide_part * all_tiles ** (-0.5)
    query_grad, score_grad, correction = query_side(
        weights, grad_blocks, key_win, value_win, scaling
    )
    key_part = product("nhqk,nqhd->nkhd", score_grad, query_blocks).reshape(
        block_count, window_area, channels
    )
    value_part = product("nhqk,nqhd->nkhd", rounded, grad_blocks).reshape(
        block_count, window_area, channels
    )
    key_full = fold_back(key_part, SIDE, REACH, block_rows, block_cols)
    value_full = fold_back(value_part, SIDE, REACH, block_rows, block_cols)
    key_sum, value_sum = return_rims(key_full, value_full)
    grad_query = unblock(query_grad.reshape(block_rows, block_cols, block_area, channels), SIDE)
    return (
        grad_query.astype(jnp.bfloat16)[None],
        key_sum.astype(jnp.bfloat16)[None],
        value_sum.astype(jnp.bfloat16)[None],
        grad_weight,
    )


def solution(mesh):
    return jax.shard_map(
        on_device,
        mesh=mesh,
        in_specs=(
            P("dp", "row", "col", None),
            P("dp", "row", "col", None),
            P("dp", "row", "col", None),
            P("dp", "row", "col"),
            P("dp", None),
            P("dp", "row", "col", None),
        ),
        out_specs=(
            P("dp", "row", "col", None),
            P("dp", "row", "col", None),
            P("dp", "row", "col", None),
            P("dp", None),
        ),
        check_vma=False,
    )
```

profile of v0, /device:TPU:39, one launch (start us, length us, event | category | flops | bytes accessed | tf_op | source)
XLA Modules:
  0.0 1018.1 jit_solution(9643661524782293680)
XLA Ops:
  7.2 1.0 slice_bitcast_fusion.5
  8.3 2.6 collective-permute-start.1
  10.9 3.1 collective-permute-start
  14.1 1.0 slice_bitcast_fusion.3
  15.0 1.9 collective-permute-start.9
  17.1 0.7 lt.64
  17.9 1.9 collective-permute-start.5
  19.8 3.6 collective-permute-start.4
  23.5 1.3 convert_convert_fusion
  24.8 0.7 convert_bitcast_fusion.2
  26.5 0.7 copy.91
  27.3 2.4 collective-permute-start.7
  29.7 8.8 collective-permute-start.6
  38.6 3.0 collective-permute-start.8
  42.2 1.9 collective-permute-start.3
  44.1 9.4 collective-permute-start.2
  53.6 1.9 collective-permute-start.11
  55.6 9.4 collective-permute-start.10
  64.9 1.4 collective-permute-done.3
  66.7 9.1 collective-permute-done.11
  76.2 0.8 slice.475
  77.5 0.8 maximum_bitcast_fusion
  78.3 0.9 reshape_reshape.22
  79.2 1.2 copy.80
  80.4 2.4 fusion.67
  82.9 1.6 bitcast_select_fusion
  85.0 0.8 maximum_bitcast_fusion.1
  85.8 0.9 reshape_reshape.25
  86.7 1.2 copy.79
  88.0 4.9 fusion.24
  93.3 0.9 reshape.537
  94.1 1.5 fusion.69
  95.6 764.2 %all-reduce.15 = bf16[768,768]{1,0:T(8,128)(2,1)} all-reduce(f32[768,768]{1,0:T(8,128)S(1)} %fusion.69), channel_id=1, replica_groups=mesh['dp'=4,'row'=8,'col'=16] {'row','col'}, use_global_device_ids=true, to_apply=%region_3.4 | all-reduce | flops 589824 | bytes 3538944 | tf_op jit(solution)/shard_map/psum | solution.py:244
  859.9 1.9 convolution_convert_fusion
  862.7 1.6 fusion.68
  864.2 11.5 %fusion.25 = bf16[2,64,12,64]{1,3,2,0:T(8,128)(2,1)} fusion(bf16[2,196,12,64]{1,3,2,0:T(8,128)(2,1)S(1)} %copy.80, f32[2,12,64,196]{3,2,1,0:T(8,128)} %fusion.68, f32[2,12,64,196]{3,2,1,0:T(8,128)} %get-tuple-element.127, f32[2,12,64]{2,1,0:T(8,128)S(1)} %broadcast_divide_fusion), kind=kOutput, calls=%fused_computation.21 | convolution fusion | flops 40742596 | bytes 3213312 | tf_op jit(solution)/shard_map/nhqk,nkhd->nqhd/dot_general | solution.py:40
  875.7 11.9 %fusion.12 = f32[2,196,12,64]{1,3,2,0:T(8,128)} fusion(bf16[2,64,12,64]{1,3,2,0:T(8,128)(2,1)S(1)} %copy-done.10, f32[2,12,64,196]{3,2,1,0:T(8,128)} %fusion.68, f32[2,12,64,196]{3,2,1,0:T(8,128)} %get-tuple-element.127, f32[2,12,64]{2,1,0:T(8,128)S(1)} %broadcast_divide_fusion), kind=kOutput, calls=%fused_computation.9 | convolution fusion | flops 40644292 | bytes 3815424 | tf_op jit(solution)/shard_map/nhqk,nqhd->nkhd/dot_general | solution.py:40
  887.7 3.5 copy.84
  891.1 2.2 reshape_reshape.26
  893.3 1.1 slice.477
  894.4 1.2 slice.476
  896.3 0.8 slice.479
  897.1 0.9 slice.478
  897.9 5.8 convolution_bitcast_fusion
  903.7 3.5 copy.87
  907.2 2.2 reshape_reshape.27
  909.4 1.1 slice.491
  910.5 1.2 slice.490
  911.6 0.5 pad_add_fusion
  912.4 0.9 copy-done.16
  914.0 0.7 copy_bitcast_fusion.2
  914.9 1.9 collective-permute-start.12
  917.1 51.0 %collective-permute-start.13 = (bf16[3,22,768]{2,1,0:T(8,128)(2,1)S(1)}, bf16[3,22,768]{2,1,0:T(8,128)(2,1)S(1)}, u32[]{:S(2)}, u32[]{:S(2)}) collective-permute-start(bf16[3,22,768]{2,1,0:T(8,128)(2,1)S(1)} %get-tuple-element.102), channel_id=1, source_target_pairs={{16,0},{32,16},{48,32},{64,48},{80,64},{96,80},{112,96},{17,1},{33... | collective-permute-start | bytes 304136 | tf_op jit(solution)/shard_map/ppermute | solution.py:15
  968.1 1.9 collective-permute-start.16
  970.0 2.4 collective-permute-start.17
  972.7 3.4 collective-permute-done.17
  976.3 9.0 collective-permute-start.14
  985.3 3.1 collective-permute-start.15
  988.5 8.2 collective-permute-start.18
  996.7 1.9 collective-permute-start.19
  999.8 7.9 collective-permute-done.19
  1008.1 0.7 convert_bitcast_fusion.1
  1008.8 0.7 convert_bitcast_fusion
  1009.5 1.8 convert_multiply_fusion
  (142 shorter events, 8.8 us)
Async XLA Ops:
  7.2 18.4 %copy-start = (bf16[1,8,16,768]{3,2,1,0:T(8,128)(2,1)S(1)}, bf16[1,8,16,768]{3,2,1,0:T(8,128)(2,1)}, u32[]{:S(2)}) copy-start(bf16[1,8,16,768]{3,2,1,0:T(8,128)(2,1)} %param.22) | copy-start | bytes 589828
  7.2 19.3 %copy-start.14 = (bf16[1,8,16,768]{3,2,1,0:T(8,128)(2,1)S(1)}, bf16[1,8,16,768]{3,2,1,0:T(8,128)(2,1)}, u32[]{:S(2)}) copy-start(bf16[1,8,16,768]{3,2,1,0:T(8,128)(2,1)} %param.27) | copy-start | bytes 589828
  7.2 852.7 %all-gather.2.cloned.1.call-start = ((), (), s32[]{:S(2)}) async-start(), calls=%async_computation.1 | async-start | bytes 1474560 | tf_op jit(solution)/shard_map/all_gather | solution.py:229
  8.3 33.8 %collective-permute-start.1 = (bf16[3,16,768]{2,1,0:T(8,128)(2,1)S(1)}, bf16[3,16,768]{2,1,0:T(8,128)(2,1)S(1)}, u32[]{:S(2)}, u32[]{:S(2)}) collective-permute-start(bf16[3,16,768]{2,1,0:T(8,128)(2,1)S(1)} %get-tuple-element.119), channel_id=1, source_target_pairs={{16,0},{32,16},{48,32},{64,48},{80,64},{96,80},{112,96},{17,1},{33... | collective-permute-start | bytes 221192 | tf_op jit(solution)/shard_map/ppermute | solution.py:32
  10.9 31.2 %collective-permute-start = (bf16[3,16,768]{2,1,0:T(8,128)(2,1)S(1)}, bf16[3,16,768]{2,1,0:T(8,128)(2,1)S(1)}, u32[]{:S(2)}, u32[]{:S(2)}) collective-permute-start(bf16[3,16,768]{2,1,0:T(8,128)(2,1)S(1)} %get-tuple-element.118), channel_id=1, source_target_pairs={{0,16},{16,32},{32,48},{48,64},{64,80},{80,96},{96,112},{1,17},{17... | collective-permute-start | bytes 221192 | tf_op jit(solution)/shard_map/ppermute | solution.py:30
  14.0 28.1 %copy-start.11 = (bf16[1,8,16,768]{3,2,1,0:T(8,128)(2,1)S(1)}, bf16[1,8,16,768]{3,2,1,0:T(8,128)(2,1)}, u32[]{:S(2)}) copy-start(bf16[1,8,16,768]{3,2,1,0:T(8,128)(2,1)} %param.23) | copy-start | bytes 589828
  14.0 995.5 %reduce-scatter.2.cloned.1.call-start = ((), (), s32[]{:S(2)}) async-start(), calls=%async_computation.2 | async-start | bytes 1474560 | tf_op jit(solution)/shard_map/reduce_scatter | solution.py:245
  15.0 38.5 %collective-permute-start.9 = (bf16[3,16,768]{2,1,0:T(8,128)(2,1)S(1)}, bf16[3,16,768]{2,1,0:T(8,128)(2,1)S(1)}, u32[]{:S(2)}, u32[]{:S(2)}) collective-permute-start(bf16[3,16,768]{2,1,0:T(8,128)(2,1)S(1)} %get-tuple-element.117), channel_id=1, source_target_pairs={{16,0},{32,16},{48,32},{64,48},{80,64},{96,80},{112,96},{17,1},{33... | collective-permute-start | bytes 221192 | tf_op jit(solution)/shard_map/ppermute | solution.py:32
  17.9 9.3 collective-permute-start.5
  19.8 7.4 collective-permute-start.4
  25.5 28.0 %copy-start.12 = (bf16[1,8,16,768]{3,2,1,0:T(8,128)(2,1)S(1)}, bf16[1,8,16,768]{3,2,1,0:T(8,128)(2,1)}, u32[]{:S(2)}) copy-start(bf16[1,8,16,768]{3,2,1,0:T(8,128)(2,1)} %param.24) | copy-start | bytes 589828
  26.3 56.6 %copy-start.9 = (bf16[2,64,12,64]{1,3,2,0:T(8,128)(2,1)}, bf16[2,64,12,64]{1,3,2,0:T(8,128)(2,1)S(1)}, u32[]{:S(2)}) copy-start(bf16[2,64,12,64]{1,3,2,0:T(8,128)(2,1)S(1)} %copy.83) | copy-start | bytes 589828
  27.3 11.3 %collective-permute-start.7 = (bf16[14,3]{1,0:T(8,128)(2,1)S(1)}, bf16[14,3]{1,0:T(8,128)(2,1)S(1)}, u32[]{:S(2)}, u32[]{:S(2)}) collective-permute-start(bf16[14,3]{1,0:T(8,128)(2,1)S(1)} %get-tuple-element.123), channel_id=1, source_target_pairs={{1,0},{2,1},{3,2},{4,3},{5,4},{6,5},{7,6},{8,7},{9,8},{10,9},{11,1... | collective-permute-start | bytes 260 | tf_op jit(solution)/shard_map/ppermute | solution.py:32
  29.7 11.8 %collective-permute-start.6 = (bf16[14,3]{1,0:T(8,128)(2,1)S(1)}, bf16[14,3]{1,0:T(8,128)(2,1)S(1)}, u32[]{:S(2)}, u32[]{:S(2)}) collective-permute-start(bf16[14,3]{1,0:T(8,128)(2,1)S(1)} %get-tuple-element.122), channel_id=1, source_target_pairs={{0,1},{1,2},{2,3},{3,4},{4,5},{5,6},{6,7},{7,8},{8,9},{9,10},{10,1... | collective-permute-start | bytes 260 | tf_op jit(solution)/shard_map/ppermute | solution.py:30
  38.6 14.9 %collective-permute-start.8 = (bf16[3,16,768]{2,1,0:T(8,128)(2,1)S(1)}, bf16[3,16,768]{2,1,0:T(8,128)(2,1)S(1)}, u32[]{:S(2)}, u32[]{:S(2)}) collective-permute-start(bf16[3,16,768]{2,1,0:T(8,128)(2,1)S(1)} %get-tuple-element.116), channel_id=1, source_target_pairs={{0,16},{16,32},{32,48},{48,64},{64,80},{80,96},{96,112},{1,17},{17... | collective-permute-start | bytes 221192 | tf_op jit(solution)/shard_map/ppermute | solution.py:30
  42.2 24.1 %collective-permute-start.3 = (bf16[14,3,768]{2,1,0:T(4,128)(2,1)S(1)}, bf16[14,3,768]{2,1,0:T(4,128)(2,1)S(1)}, u32[]{:S(2)}, u32[]{:S(2)}) collective-permute-start(bf16[14,3,768]{2,1,0:T(4,128)(2,1)S(1)} %get-tuple-element.111), channel_id=1, source_target_pairs={{1,0},{2,1},{3,2},{4,3},{5,4},{6,5},{7,6},{8,7},{9,8},{10,9},{11,1... | collective-permute-start | bytes 193544 | tf_op jit(solution)/shard_map/ppermute | solution.py:32
  44.1 22.2 %collective-permute-start.2 = (bf16[14,3,768]{2,1,0:T(4,128)(2,1)S(1)}, bf16[14,3,768]{2,1,0:T(4,128)(2,1)S(1)}, u32[]{:S(2)}, u32[]{:S(2)}) collective-permute-start(bf16[14,3,768]{2,1,0:T(4,128)(2,1)S(1)} %get-tuple-element.110), channel_id=1, source_target_pairs={{0,1},{1,2},{2,3},{3,4},{4,5},{5,6},{6,7},{7,8},{8,9},{9,10},{10,1... | collective-permute-start | bytes 193544 | tf_op jit(solution)/shard_map/ppermute | solution.py:30
  53.6 22.2 %collective-permute-start.11 = (bf16[14,3,768]{2,1,0:T(4,128)(2,1)S(1)}, bf16[14,3,768]{2,1,0:T(4,128)(2,1)S(1)}, u32[]{:S(2)}, u32[]{:S(2)}) collective-permute-start(bf16[14,3,768]{2,1,0:T(4,128)(2,1)S(1)} %get-tuple-element.109), channel_id=1, source_target_pairs={{1,0},{2,1},{3,2},{4,3},{5,4},{6,5},{7,6},{8,7},{9,8},{10,9},{11,1... | collective-permute-start | bytes 193544 | tf_op jit(solution)/shard_map/ppermute | solution.py:32
  55.6 20.3 %collective-permute-start.10 = (bf16[14,3,768]{2,1,0:T(4,128)(2,1)S(1)}, bf16[14,3,768]{2,1,0:T(4,128)(2,1)S(1)}, u32[]{:S(2)}, u32[]{:S(2)}) collective-permute-start(bf16[14,3,768]{2,1,0:T(4,128)(2,1)S(1)} %get-tuple-element.108), channel_id=1, source_target_pairs={{0,1},{1,2},{2,3},{3,4},{4,5},{5,6},{6,7},{7,8},{8,9},{9,10},{10,1... | collective-permute-start | bytes 193544 | tf_op jit(solution)/shard_map/ppermute | solution.py:30
  66.7 9.4 copy-start.5
  76.1 1.1 slice-start
  76.2 2.0 copy-start.6
  82.9 1.6 copy-start.13
  82.9 1.8 slice-start.1
  86.7 1.2 copy-start.18
  87.9 5.3 copy-start.3
  95.6 764.3 %copy-start.15 = (bf16[1,8,16,768]{3,2,1,0:T(8,128)(2,1)S(1)}, bf16[1,8,16,768]{3,2,1,0:T(8,128)(2,1)}, u32[]{:S(2)}) copy-start(bf16[1,8,16,768]{3,2,1,0:T(8,128)(2,1)} %param.27) | copy-start | bytes 589828
  859.9 2.0 copy-start.17
  859.9 2.7 copy-start.4
  862.7 13.1 %copy-start.1 = (bf16[2,64,12,64]{1,3,2,0:T(8,128)(2,1)}, bf16[2,64,12,64]{1,3,2,0:T(8,128)(2,1)S(1)}, u32[]{:S(2)}) copy-start(bf16[2,64,12,64]{1,3,2,0:T(8,128)(2,1)S(1)} %copy.86) | copy-start | bytes 589828
  864.2 11.5 %copy-start.10 = (bf16[2,64,12,64]{1,3,2,0:T(8,128)(2,1)S(1)}, bf16[2,64,12,64]{1,3,2,0:T(8,128)(2,1)}, u32[]{:S(2)}) copy-start(bf16[2,64,12,64]{1,3,2,0:T(8,128)(2,1)} %copy-done.9) | copy-start | bytes 589828
  896.3 1.7 copy-start.2
  912.3 1.0 copy-start.16
  912.4 2.4 copy-start.7
  912.4 2.4 copy-start.8
  914.9 57.5 %collective-permute-start.12 = (bf16[3,22,768]{2,1,0:T(8,128)(2,1)S(1)}, bf16[3,22,768]{2,1,0:T(8,128)(2,1)S(1)}, u32[]{:S(2)}, u32[]{:S(2)}) collective-permute-start(bf16[3,22,768]{2,1,0:T(8,128)(2,1)S(1)} %get-tuple-element.103), channel_id=1, source_target_pairs={{0,16},{16,32},{32,48},{48,64},{64,80},{80,96},{96,112},{1,17},{17... | collective-permute-start | bytes 304136 | tf_op jit(solution)/shard_map/ppermute | solution.py:15
  917.1 55.4 %collective-permute-start.13 = (bf16[3,22,768]{2,1,0:T(8,128)(2,1)S(1)}, bf16[3,22,768]{2,1,0:T(8,128)(2,1)S(1)}, u32[]{:S(2)}, u32[]{:S(2)}) collective-permute-start(bf16[3,22,768]{2,1,0:T(8,128)(2,1)S(1)} %get-tuple-element.102), channel_id=1, source_target_pairs={{16,0},{32,16},{48,32},{64,48},{80,64},{96,80},{112,96},{17,1},{33... | collective-permute-start | bytes 304136 | tf_op jit(solution)/shard_map/ppermute | solution.py:15
  968.1 4.4 collective-permute-start.16
  970.0 6.1 collective-permute-start.17
  976.3 22.3 %collective-permute-start.14 = (bf16[8,3,768]{2,1,0:T(4,128)(2,1)S(1)}, bf16[8,3,768]{2,1,0:T(4,128)(2,1)S(1)}, u32[]{:S(2)}, u32[]{:S(2)}) collective-permute-start(bf16[8,3,768]{2,1,0:T(4,128)(2,1)S(1)} %get-tuple-element.115), channel_id=1, source_target_pairs={{0,1},{1,2},{2,3},{3,4},{4,5},{5,6},{6,7},{7,8},{8,9},{9,10},{10,1... | collective-permute-start | bytes 110600 | tf_op jit(solution)/shard_map/ppermute | solution.py:15
  985.3 13.8 %collective-permute-start.15 = (bf16[8,3,768]{2,1,0:T(4,128)(2,1)S(1)}, bf16[8,3,768]{2,1,0:T(4,128)(2,1)S(1)}, u32[]{:S(2)}, u32[]{:S(2)}) collective-permute-start(bf16[8,3,768]{2,1,0:T(4,128)(2,1)S(1)} %get-tuple-element.114), channel_id=1, source_target_pairs={{1,0},{2,1},{3,2},{4,3},{5,4},{6,5},{7,6},{8,7},{9,8},{10,9},{11,1... | collective-permute-start | bytes 110600 | tf_op jit(solution)/shard_map/ppermute | solution.py:15
  988.5 10.2 collective-permute-start.18
  996.7 11.1 %collective-permute-start.19 = (bf16[8,3,768]{2,1,0:T(4,128)(2,1)S(1)}, bf16[8,3,768]{2,1,0:T(4,128)(2,1)S(1)}, u32[]{:S(2)}, u32[]{:S(2)}) collective-permute-start(bf16[8,3,768]{2,1,0:T(4,128)(2,1)S(1)} %get-tuple-element.112), channel_id=1, source_target_pairs={{1,0},{2,1},{3,2},{4,3},{5,4},{6,5},{7,6},{8,7},{9,8},{10,9},{11,1... | collective-permute-start | bytes 110600 | tf_op jit(solution)/shard_map/ppermute | solution.py:15
Sparse Core Ops, SparseCore 0:
  14.1 41.7 all-gather.1
  860.0 89.8 reduce-scatter.1
where the time goes:
time: 1020 us
  blocking collectives  764 us (75%)
  starting transfers between devices  130 us (13%)
  matrix products  43 us (4%)
  local copies, waits for them, and re-layouts  35 us (3%)
  waiting for transfers between devices  21.9 us (2%)
  between operations  15.1 us (1%)
    psum x1, blocking collectives, on_device(): summed = lax.psum(weight_term, ('row', 'col'))  764 us
    ppermute x8, starting transfers between devices, passed_along(): lax.ppermute(value, axis, [(source, source + steps) for source in range(l...  79.4 us
    ppermute x6, starting transfers between devices, extended(): lax.ppermute(tail, axis, [(i, (i + 1) % count) for i in range(ends)])  37.3 us
    dot_general x6, matrix products, product(): return jnp.einsum(form, left, right, preferred_element_type=jnp.float32)  37.2 us
  transfers between devices with their start and end apart: 22, of which 4 were waited for; matrix products, arithmetic and copies ran while one was open for 8% of the time, Pallas kernels for 0%

commit v1 on v0

--- a/solution.py
+++ b/solution.py
@@ -241,7 +241,7 @@
         (((0,), (0,)), ((), ())),
         preferred_element_type=jnp.float32,
     )
-    summed = lax.psum(weight_term, ("row", "col"))
+    summed = lax.psum(lax.psum(weight_term, "col"), "row")
     slide_part = lax.psum_scatter(
         summed.astype(jnp.bfloat16), "dp", scatter_dimension=0, tiled=True
     ).astype(jnp.float32)

time: 1020 us -> 479 us (0.47)
  the two profiles are of different devices: /device:TPU:39 before, /device:TPU:1 now
where the time goes in v1:
time: 479 us; the launch traced here: 478 us
  waiting for transfers between devices  256 us (53%)
  blocking collectives  62.1 us (13%)
  starting transfers between devices  56.4 us (12%)
  matrix products  39.4 us (8%)
  local copies, waits for them, and re-layouts  37.4 us (8%)
  between operations  16.5 us (3%)
  other arithmetic  9.72 us (2%)
    psum x1, waiting for transfers between devices, on_device(): summed = lax.psum(lax.psum(weight_term, 'col'), 'row')  228 us
    psum x1, blocking collectives, on_device(): summed = lax.psum(lax.psum(weight_term, 'col'), 'row')  62.1 us
    dot_general x6, matrix products, product(): return jnp.einsum(form, left, right, preferred_element_type=jnp.float32)  32.8 us
    reduce_scatter x1, waiting for transfers between devices, on_device(): lax.psum_scatter(summed.astype(jnp.bfloat16), 'dp', scatter_dimension=0,...  24.9 us
    ppermute x6, starting transfers between devices, extended(): lax.ppermute(tail, axis, [(i, (i + 1) % count) for i in range(ends)])  20 us
    ppermute x8, starting transfers between devices, passed_along(): lax.ppermute(value, axis, [(source, source + steps) for source in range(l...  19.2 us
    ppermute x6, starting transfers between devices, extended(): lax.ppermute(head, axis, [((i + 1) % count, i) for i in range(ends)])  16.9 us
  transfers between devices with their start and end apart: 23, of which 4 were waited for; matrix products, arithmetic and copies ran while one was open for 17% of the time, Pallas kernels for 0%

profile of v1, /device:TPU:1, one launch (start us, length us, event | category | flops | bytes accessed | tf_op | source)
XLA Modules:
  0.0 477.6 jit_solution(6057512787554124429)
XLA Ops:
  8.1 1.0 slice_bitcast_fusion.5
  9.1 8.7 %collective-permute-start.1 = (bf16[3,16,768]{2,1,0:T(8,128)(2,1)S(1)}, bf16[3,16,768]{2,1,0:T(8,128)(2,1)S(1)}, u32[]{:S(2)}, u32[]{:S(2)}) collective-permute-start(bf16[3,16,768]{2,1,0:T(8,128)(2,1)S(1)} %get-tuple-element.119), channel_id=1, source_target_pairs={{16,0},{32,16},{48,32},{64,48},{80,64},{96,80},{112,96},{17,1},{33... | collective-permute-start | bytes 221192 | tf_op jit(solution)/shard_map/ppermute | solution.py:32
  17.9 1.9 collective-permute-start
  19.9 1.0 slice_bitcast_fusion.3
  20.8 2.4 collective-permute-start.9
  23.4 0.7 lt.64
  24.2 1.9 collective-permute-start.5
  26.1 3.6 collective-permute-start.4
  29.8 0.7 convert_convert_fusion
  30.5 0.7 convert_bitcast_fusion.2
  31.6 1.1 copy.83
  32.9 0.7 copy.91
  33.7 1.3 collective-permute-start.7
  35.0 4.0 collective-permute-start.6
  39.0 2.5 collective-permute-start.8
  42.1 1.3 collective-permute-start.3
  43.4 4.0 collective-permute-start.2
  47.5 1.3 collective-permute-start.11
  48.8 4.0 collective-permute-start.10
  53.1 1.2 collective-permute-done.10
  55.3 0.8 maximum_bitcast_fusion
  56.1 0.9 reshape_reshape.22
  57.1 1.2 copy.80
  58.8 0.8 maximum_bitcast_fusion.1
  59.6 0.9 reshape_reshape.25
  60.5 1.2 copy.79
  61.7 2.9 fusion.67
  64.6 1.4 bitcast_select_fusion
  66.1 3.5 fusion.24
  69.6 1.4 copy.90
  71.2 1.9 fusion.69
  74.0 1.8 convolution_convert_fusion
  77.4 0.8 copy-done.10
  78.3 10.9 %fusion.12 = f32[2,196,12,64]{1,3,2,0:T(8,128)} fusion(bf16[2,64,12,64]{1,3,2,0:T(8,128)(2,1)S(1)} %copy-done.11, f32[2,12,64,196]{3,2,1,0:T(8,128)S(1)} %fusion.68, f32[2,12,64,196]{3,2,1,0:T(8,128)} %get-tuple-element.127, f32[2,12,64]{2,1,0:T(8,128)S(1)} %broadcast_divide_fusion), kind=kOutput, calls=%fused_computation.9 | convolution fusion | flops 40644292 | bytes 3815424 | tf_op jit(solution)/shard_map/nhqk,nqhd->nkhd/dot_general | solution.py:40
  89.2 3.5 copy.84
  92.7 2.2 reshape_reshape.26
  94.9 1.1 slice.477
  96.0 1.2 slice.476
  97.8 0.8 slice.479
  98.6 0.9 slice.478
  99.5 5.8 %convolution_bitcast_fusion = f32[2,196,12,64]{1,3,2,0:T(8,128)} fusion(bf16[2,64,12,64]{1,3,2,0:T(8,128)(2,1)S(1)} %copy-done.2, f32[2,12,64]{2,1,0:T(8,128)S(1)} %broadcast_divide_fusion, f32[2,12,64,196]{3,2,1,0:T(8,128)} %copy-done.7), kind=kOutput, calls=%fused_computation.11 | convolution fusion | flops 39440068 | bytes 2611200 | tf_op jit(solution)/shard_map/nhqk,nqhd->nkhd/dot_general | solution.py:40
  105.3 3.5 copy.87
  108.8 2.2 reshape_reshape.27
  111.0 1.1 slice.491
  112.1 1.2 slice.490
  113.9 0.8 slice.493
  115.2 10.7 %fusion.25 = bf16[2,64,12,64]{1,3,2,0:T(8,128)(2,1)S(1)} fusion(bf16[2,196,12,64]{1,3,2,0:T(8,128)(2,1)S(1)} %copy-done.4, f32[2,12,64,196]{3,2,1,0:T(8,128)} %copy-done.10, f32[2,12,64,196]{3,2,1,0:T(8,128)} %get-tuple-element.127, f32[2,12,64]{2,1,0:T(8,128)S(1)} %broadcast_divide_fusion), kind=kOutput, calls=%fused_computation.21 | convolution fusion | flops 40742596 | bytes 3213312 | tf_op jit(solution)/shard_map/nhqk,nkhd->nqhd/dot_general | solution.py:40
  127.0 3.8 collective-permute-start.12
  130.8 1.9 collective-permute-start.13
  132.8 0.7 copy_bitcast_fusion.2
  133.7 3.6 collective-permute-start.16
  137.3 1.9 collective-permute-start.17
  139.3 227.5 %all-reduce.17.cloned.1.call-done = f32[768,768]{1,0:T(8,128)} async-done(((f32[768,768]{1,0:T(8,128)}), f32[768,768]{1,0:T(8,128)}) %all-reduce.17.cloned.1.call-update) | async-done | bytes 2359312 | tf_op jit(solution)/shard_map/psum | solution.py:244
  366.8 62.1 %all-reduce.18 = bf16[768,768]{1,0:T(8,128)(2,1)} all-reduce(f32[768,768]{1,0:T(8,128)} %all-reduce.17.cloned.1.call-done), channel_id=1, replica_groups=mesh['dp'=4,'row'=8,'col'=16] {'row'}, use_global_device_ids=true, to_apply=%region_4.5 | all-reduce | flops 589824 | bytes 3538944 | tf_op jit(solution)/shard_map/psum | solution.py:244
  429.0 0.9 fusion.46
  430.2 1.3 collective-permute-start.14
  431.5 1.3 collective-permute-start.15
  432.9 4.0 collective-permute-start.18
  436.9 1.3 collective-permute-start.19
  439.4 2.3 collective-permute-done.19
  442.0 0.7 convert_bitcast_fusion.1
  442.7 0.7 convert_bitcast_fusion
  443.4 24.9 %reduce-scatter.2.cloned.1.call-done = bf16[192,768]{1,0:T(8,128)(2,1)} async-done(((bf16[768,768]{1,0:T(8,128)(2,1)}), bf16[192,768]{1,0:T(8,128)(2,1)}) %reduce-scatter.2.cloned.1.call-update) | async-done | bytes 294928 | tf_op jit(solution)/shard_map/reduce_scatter | solution.py:245
  468.4 1.8 convert_multiply_fusion
  (140 shorter events, 10.7 us)
Async XLA Ops:
  8.0 23.2 %copy-start = (bf16[1,8,16,768]{3,2,1,0:T(8,128)(2,1)S(1)}, bf16[1,8,16,768]{3,2,1,0:T(8,128)(2,1)}, u32[]{:S(2)}) copy-start(bf16[1,8,16,768]{3,2,1,0:T(8,128)(2,1)} %param.22) | copy-start | bytes 589828
  8.0 24.9 %copy-start.14 = (bf16[1,8,16,768]{3,2,1,0:T(8,128)(2,1)S(1)}, bf16[1,8,16,768]{3,2,1,0:T(8,128)(2,1)}, u32[]{:S(2)}) copy-start(bf16[1,8,16,768]{3,2,1,0:T(8,128)(2,1)} %param.27) | copy-start | bytes 589828
  8.0 65.3 %all-gather.2.cloned.1.call-start = ((), (), s32[]{:S(2)}) async-start(), calls=%async_computation.1 | async-start | bytes 1474560 | tf_op jit(solution)/shard_map/all_gather | solution.py:229
  9.1 32.9 %collective-permute-start.1 = (bf16[3,16,768]{2,1,0:T(8,128)(2,1)S(1)}, bf16[3,16,768]{2,1,0:T(8,128)(2,1)S(1)}, u32[]{:S(2)}, u32[]{:S(2)}) collective-permute-start(bf16[3,16,768]{2,1,0:T(8,128)(2,1)S(1)} %get-tuple-element.119), channel_id=1, source_target_pairs={{16,0},{32,16},{48,32},{64,48},{80,64},{96,80},{112,96},{17,1},{33... | collective-permute-start | bytes 221192 | tf_op jit(solution)/shard_map/ppermute | solution.py:32
  17.9 24.2 %collective-permute-start = (bf16[3,16,768]{2,1,0:T(8,128)(2,1)S(1)}, bf16[3,16,768]{2,1,0:T(8,128)(2,1)S(1)}, u32[]{:S(2)}, u32[]{:S(2)}) collective-permute-start(bf16[3,16,768]{2,1,0:T(8,128)(2,1)S(1)} %get-tuple-element.118), channel_id=1, source_target_pairs={{0,16},{16,32},{32,48},{48,64},{64,80},{80,96},{96,112},{1,17},{17... | collective-permute-start | bytes 221192 | tf_op jit(solution)/shard_map/ppermute | solution.py:30
  19.8 22.2 %copy-start.12 = (bf16[1,8,16,768]{3,2,1,0:T(8,128)(2,1)S(1)}, bf16[1,8,16,768]{3,2,1,0:T(8,128)(2,1)}, u32[]{:S(2)}) copy-start(bf16[1,8,16,768]{3,2,1,0:T(8,128)(2,1)} %param.23) | copy-start | bytes 589828
  19.8 347.0 %all-reduce.17.cloned.1.call-start = ((), (), s32[]{:S(2)}) async-start(), calls=%async_computation.2 | async-start | bytes 4718592 | tf_op jit(solution)/shard_map/psum | solution.py:244
  20.8 26.6 %collective-permute-start.9 = (bf16[3,16,768]{2,1,0:T(8,128)(2,1)S(1)}, bf16[3,16,768]{2,1,0:T(8,128)(2,1)S(1)}, u32[]{:S(2)}, u32[]{:S(2)}) collective-permute-start(bf16[3,16,768]{2,1,0:T(8,128)(2,1)S(1)} %get-tuple-element.117), channel_id=1, source_target_pairs={{16,0},{32,16},{48,32},{64,48},{80,64},{96,80},{112,96},{17,1},{33... | collective-permute-start | bytes 221192 | tf_op jit(solution)/shard_map/ppermute | solution.py:32
  24.2 9.4 %collective-permute-start.5 = (bf16[3,16]{1,0:T(4,128)(2,1)S(1)}, bf16[3,16]{1,0:T(4,128)(2,1)S(1)}, u32[]{:S(2)}, u32[]{:S(2)}) collective-permute-start(bf16[3,16]{1,0:T(4,128)(2,1)S(1)} %get-tuple-element.125), channel_id=1, source_target_pairs={{16,0},{32,16},{48,32},{64,48},{80,64},{96,80},{112,96},{17,1},{33... | collective-permute-start | bytes 296 | tf_op jit(solution)/shard_map/ppermute | solution.py:32
  26.1 7.5 %collective-permute-start.4 = (bf16[3,16]{1,0:T(4,128)(2,1)S(1)}, bf16[3,16]{1,0:T(4,128)(2,1)S(1)}, u32[]{:S(2)}, u32[]{:S(2)}) collective-permute-start(bf16[3,16]{1,0:T(4,128)(2,1)S(1)} %get-tuple-element.124), channel_id=1, source_target_pairs={{0,16},{16,32},{32,48},{48,64},{64,80},{80,96},{96,112},{1,17},{17... | collective-permute-start | bytes 296 | tf_op jit(solution)/shard_map/ppermute | solution.py:30
  31.2 16.2 %copy-start.13 = (bf16[1,8,16,768]{3,2,1,0:T(8,128)(2,1)S(1)}, bf16[1,8,16,768]{3,2,1,0:T(8,128)(2,1)}, u32[]{:S(2)}) copy-start(bf16[1,8,16,768]{3,2,1,0:T(8,128)(2,1)} %param.24) | copy-start | bytes 589828
  33.7 5.3 %collective-permute-start.7 = (bf16[14,3]{1,0:T(8,128)(2,1)S(1)}, bf16[14,3]{1,0:T(8,128)(2,1)S(1)}, u32[]{:S(2)}, u32[]{:S(2)}) collective-permute-start(bf16[14,3]{1,0:T(8,128)(2,1)S(1)} %get-tuple-element.123), channel_id=1, source_target_pairs={{1,0},{2,1},{3,2},{4,3},{5,4},{6,5},{7,6},{8,7},{9,8},{10,9},{11,1... | collective-permute-start | bytes 260 | tf_op jit(solution)/shard_map/ppermute | solution.py:32
  35.0 6.5 %collective-permute-start.6 = (bf16[14,3]{1,0:T(8,128)(2,1)S(1)}, bf16[14,3]{1,0:T(8,128)(2,1)S(1)}, u32[]{:S(2)}, u32[]{:S(2)}) collective-permute-start(bf16[14,3]{1,0:T(8,128)(2,1)S(1)} %get-tuple-element.122), channel_id=1, source_target_pairs={{0,1},{1,2},{2,3},{3,4},{4,5},{5,6},{6,7},{7,8},{8,9},{9,10},{10,1... | collective-permute-start | bytes 260 | tf_op jit(solution)/shard_map/ppermute | solution.py:30
  39.0 8.4 %collective-permute-start.8 = (bf16[3,16,768]{2,1,0:T(8,128)(2,1)S(1)}, bf16[3,16,768]{2,1,0:T(8,128)(2,1)S(1)}, u32[]{:S(2)}, u32[]{:S(2)}) collective-permute-start(bf16[3,16,768]{2,1,0:T(8,128)(2,1)S(1)} %get-tuple-element.116), channel_id=1, source_target_pairs={{0,16},{16,32},{32,48},{48,64},{64,80},{80,96},{96,112},{1,17},{17... | collective-permute-start | bytes 221192 | tf_op jit(solution)/shard_map/ppermute | solution.py:30
  42.1 10.7 %collective-permute-start.3 = (bf16[14,3,768]{2,1,0:T(4,128)(2,1)S(1)}, bf16[14,3,768]{2,1,0:T(4,128)(2,1)S(1)}, u32[]{:S(2)}, u32[]{:S(2)}) collective-permute-start(bf16[14,3,768]{2,1,0:T(4,128)(2,1)S(1)} %get-tuple-element.111), channel_id=1, source_target_pairs={{1,0},{2,1},{3,2},{4,3},{5,4},{6,5},{7,6},{8,7},{9,8},{10,9},{11,1... | collective-permute-start | bytes 193544 | tf_op jit(solution)/shard_map/ppermute | solution.py:32
  43.4 9.4 %collective-permute-start.2 = (bf16[14,3,768]{2,1,0:T(4,128)(2,1)S(1)}, bf16[14,3,768]{2,1,0:T(4,128)(2,1)S(1)}, u32[]{:S(2)}, u32[]{:S(2)}) collective-permute-start(bf16[14,3,768]{2,1,0:T(4,128)(2,1)S(1)} %get-tuple-element.110), channel_id=1, source_target_pairs={{0,1},{1,2},{2,3},{3,4},{4,5},{5,6},{6,7},{7,8},{8,9},{9,10},{10,1... | collective-permute-start | bytes 193544 | tf_op jit(solution)/shard_map/ppermute | solution.py:30
  47.5 5.6 %collective-permute-start.11 = (bf16[14,3,768]{2,1,0:T(4,128)(2,1)S(1)}, bf16[14,3,768]{2,1,0:T(4,128)(2,1)S(1)}, u32[]{:S(2)}, u32[]{:S(2)}) collective-permute-start(bf16[14,3,768]{2,1,0:T(4,128)(2,1)S(1)} %get-tuple-element.109), channel_id=1, source_target_pairs={{1,0},{2,1},{3,2},{4,3},{5,4},{6,5},{7,6},{8,7},{9,8},{10,9},{11,1... | collective-permute-start | bytes 193544 | tf_op jit(solution)/shard_map/ppermute | solution.py:32
  48.8 5.5 %collective-permute-start.10 = (bf16[14,3,768]{2,1,0:T(4,128)(2,1)S(1)}, bf16[14,3,768]{2,1,0:T(4,128)(2,1)S(1)}, u32[]{:S(2)}, u32[]{:S(2)}) collective-permute-start(bf16[14,3,768]{2,1,0:T(4,128)(2,1)S(1)} %get-tuple-element.108), channel_id=1, source_target_pairs={{0,1},{1,2},{2,3},{3,4},{4,5},{5,6},{6,7},{7,8},{8,9},{9,10},{10,1... | collective-permute-start | bytes 193544 | tf_op jit(solution)/shard_map/ppermute | solution.py:30
  54.8 1.3 copy-start.5
  57.1 1.4 slice-start
  58.3 6.3 %copy-start.3 = (bf16[2,196,12,64]{1,3,2,0:T(8,128)(2,1)}, bf16[2,196,12,64]{1,3,2,0:T(8,128)(2,1)S(1)}, u32[]{:S(2)}) copy-start(bf16[2,196,12,64]{1,3,2,0:T(8,128)(2,1)S(1)} %copy.80) | copy-start | bytes 1806340
  66.1 4.9 %copy-start.7 = (f32[2,12,64,196]{3,2,1,0:T(8,128)}, f32[2,12,64,196]{3,2,1,0:T(8,128)S(1)}, u32[]{:S(2)}) copy-start(f32[2,12,64,196]{3,2,1,0:T(8,128)S(1)} %bitcast_select_fusion) | copy-start | bytes 3612676
  66.1 5.1 %copy-start.16 = (bf16[1,2,8,8,768]{4,3,2,1,0:T(8,128)(2,1)S(1)}, bf16[1,2,8,8,768]{4,3,2,1,0:T(8,128)(2,1)}, u32[]{:S(2)}) copy-start(bf16[1,2,8,8,768]{4,3,2,1,0:T(8,128)(2,1)} %copy.91) | copy-start | bytes 589828
  73.1 0.9 copy-start.15
  73.1 395.3 %reduce-scatter.2.cloned.1.call-start = ((), (), s32[]{:S(2)}) async-start(), calls=%async_computation.3 | async-start | bytes 1474560 | tf_op jit(solution)/shard_map/reduce_scatter | solution.py:245
  76.7 0.8 copy-start.1
  76.7 1.6 copy-start.11
  77.1 1.2 copy-start.10
  97.8 1.7 copy-start.2
  113.9 1.3 copy-start.4
  115.2 11.5 %copy-start.6 = (f32[1,8,22,768]{3,2,1,0:T(8,128)S(1)}, f32[1,8,22,768]{3,2,1,0:T(8,128)}, u32[]{:S(2)}) copy-start(f32[1,8,22,768]{3,2,1,0:T(8,128)} %slice.478) | copy-start | bytes 1622020
  115.2 11.5 %copy-start.8 = (f32[1,6,22,768]{3,2,1,0:T(8,128)S(1)}, f32[1,6,22,768]{3,2,1,0:T(8,128)}, u32[]{:S(2)}) copy-start(f32[1,6,22,768]{3,2,1,0:T(8,128)} %slice.479) | copy-start | bytes 1216516
  126.8 5.9 %copy-start.9 = (f32[1,6,22,768]{3,2,1,0:T(8,128)S(1)}, f32[1,6,22,768]{3,2,1,0:T(8,128)}, u32[]{:S(2)}) copy-start(f32[1,6,22,768]{3,2,1,0:T(8,128)} %slice.493) | copy-start | bytes 1216516
  127.0 12.3 %collective-permute-start.12 = (bf16[3,22,768]{2,1,0:T(8,128)(2,1)S(1)}, bf16[3,22,768]{2,1,0:T(8,128)(2,1)S(1)}, u32[]{:S(2)}, u32[]{:S(2)}) collective-permute-start(bf16[3,22,768]{2,1,0:T(8,128)(2,1)S(1)} %get-tuple-element.103), channel_id=1, source_target_pairs={{0,16},{16,32},{32,48},{48,64},{64,80},{80,96},{96,112},{1,17},{17... | collective-permute-start | bytes 304136 | tf_op jit(solution)/shard_map/ppermute | solution.py:15
  130.8 298.1 %collective-permute-start.13 = (bf16[3,22,768]{2,1,0:T(8,128)(2,1)S(1)}, bf16[3,22,768]{2,1,0:T(8,128)(2,1)}, u32[]{:S(2)}, u32[]{:S(2)}) collective-permute-start(bf16[3,22,768]{2,1,0:T(8,128)(2,1)S(1)} %get-tuple-element.102), channel_id=1, source_target_pairs={{16,0},{32,16},{48,32},{64,48},{80,64},{96,80},{112,96},{17,1},{33... | collective-permute-start | bytes 304136 | tf_op jit(solution)/shard_map/ppermute | solution.py:15
  133.7 296.2 %collective-permute-start.16 = (bf16[3,22,768]{2,1,0:T(8,128)(2,1)S(1)}, bf16[3,22,768]{2,1,0:T(8,128)(2,1)S(1)}, u32[]{:S(2)}, u32[]{:S(2)}) collective-permute-start(bf16[3,22,768]{2,1,0:T(8,128)(2,1)S(1)} %get-tuple-element.101), channel_id=1, source_target_pairs={{0,16},{16,32},{32,48},{48,64},{64,80},{80,96},{96,112},{1,17},{17... | collective-permute-start | bytes 304136 | tf_op jit(solution)/shard_map/ppermute | solution.py:15
  137.3 292.7 %collective-permute-start.17 = (bf16[3,22,768]{2,1,0:T(8,128)(2,1)S(1)}, bf16[3,22,768]{2,1,0:T(8,128)(2,1)S(1)}, u32[]{:S(2)}, u32[]{:S(2)}) collective-permute-start(bf16[3,22,768]{2,1,0:T(8,128)(2,1)S(1)} %get-tuple-element.100), channel_id=1, source_target_pairs={{16,0},{32,16},{48,32},{64,48},{80,64},{96,80},{112,96},{17,1},{33... | collective-permute-start | bytes 304136 | tf_op jit(solution)/shard_map/ppermute | solution.py:15
  430.2 8.0 %collective-permute-start.14 = (bf16[8,3,768]{2,1,0:T(4,128)(2,1)S(1)}, bf16[8,3,768]{2,1,0:T(4,128)(2,1)S(1)}, u32[]{:S(2)}, u32[]{:S(2)}) collective-permute-start(bf16[8,3,768]{2,1,0:T(4,128)(2,1)S(1)} %get-tuple-element.115), channel_id=1, source_target_pairs={{0,1},{1,2},{2,3},{3,4},{4,5},{5,6},{6,7},{7,8},{8,9},{9,10},{10,1... | collective-permute-start | bytes 110600 | tf_op jit(solution)/shard_map/ppermute | solution.py:15
  431.5 7.1 %collective-permute-start.15 = (bf16[8,3,768]{2,1,0:T(4,128)(2,1)S(1)}, bf16[8,3,768]{2,1,0:T(4,128)(2,1)S(1)}, u32[]{:S(2)}, u32[]{:S(2)}) collective-permute-start(bf16[8,3,768]{2,1,0:T(4,128)(2,1)S(1)} %get-tuple-element.114), channel_id=1, source_target_pairs={{1,0},{2,1},{3,2},{4,3},{5,4},{6,5},{7,6},{8,7},{9,8},{10,9},{11,1... | collective-permute-start | bytes 110600 | tf_op jit(solution)/shard_map/ppermute | solution.py:15
  432.9 5.4 %collective-permute-start.18 = (bf16[8,3,768]{2,1,0:T(4,128)(2,1)S(1)}, bf16[8,3,768]{2,1,0:T(4,128)(2,1)S(1)}, u32[]{:S(2)}, u32[]{:S(2)}) collective-permute-start(bf16[8,3,768]{2,1,0:T(4,128)(2,1)S(1)} %get-tuple-element.113), channel_id=1, source_target_pairs={{0,1},{1,2},{2,3},{3,4},{4,5},{5,6},{6,7},{7,8},{8,9},{9,10},{10,1... | collective-permute-start | bytes 110600 | tf_op jit(solution)/shard_map/ppermute | solution.py:15
  436.9 4.8 %collective-permute-start.19 = (bf16[8,3,768]{2,1,0:T(4,128)(2,1)S(1)}, bf16[8,3,768]{2,1,0:T(4,128)(2,1)S(1)}, u32[]{:S(2)}, u32[]{:S(2)}) collective-permute-start(bf16[8,3,768]{2,1,0:T(4,128)(2,1)S(1)} %get-tuple-element.112), channel_id=1, source_target_pairs={{1,0},{2,1},{3,2},{4,3},{5,4},{6,5},{7,6},{8,7},{9,8},{10,9},{11,1... | collective-permute-start | bytes 110600 | tf_op jit(solution)/shard_map/ppermute | solution.py:15
Sparse Core Ops, SparseCore 0:
  19.9 43.1 all-gather.1
  429.1 39.2 reduce-scatter.1
Sparse Core Ops, SparseCore 1:
  73.2 293.6 all-reduce.16
